TPU v7x, 32 devices: a whole 2x2x4 slice. The times are simulated.
32 devices in a mesh: row: 4 (over y, x), col: 8 (over z, core).
Axes of the slice: x: 2, y: 2, z: 4, core: 2. Of those that a mesh axis runs over, the one named last changes fastest.
Arguments:
- rhs: float32 [1536, 3072], P('row', 'col'), may hold values from -6 to 6
- a_coupling: bfloat16 [3, 1536, 3072], P(None, 'row', 'col'), may hold values from -0.3125 to 0.3125
- b_coupling: bfloat16 [3, 1536, 3072], P(None, 'row', 'col'), may hold values from -0.3125 to 0.3125
- a_basis: float32 [1536, 384], P('row'), may hold values from -0.3125 to 0.3125
- b_basis: float32 [3072, 384], P('col'), may hold values from -0.3125 to 0.3125
- a_vals: float32 [1536], P('row'), may hold values from 0.25 to 4
- b_vals: float32 [3072], P('col'), may hold values from 0.25 to 4
Outputs:
- solution: bfloat16 [1536, 3072], P('row', 'col')
- rhs_next: float32 [1536, 3072], P('row', 'col')
All inputs are finite; a program needn't handle non-finite values.
Results may differ from a plain program's by a relative error of at most 0.0037.
Values may be sent and summed in bfloat16 or wider, within the bound.
No kernel may reach another device: no remote copies, remote signals or barrier semaphores. Data moves between devices by JAX's collectives and lax.ppermute only.
A program may use at most 64 MiB of HBM per device.

v0:
```python
import jax
import jax.numpy as jnp
from jax import lax
from jax.sharding import PartitionSpec as P


def carried_in(part, axis, combine, identity, reverse):
    count = lax.axis_size(axis)
    place = lax.axis_index(axis)
    ahead = count - 1 - place if reverse else place
    gathered = lax.all_gather(part, axis)
    state = jnp.zeros_like(part) + jnp.asarray(identity, part.dtype)

    def one(lap, state):
        source = count - 1 - lap if reverse else lap
        return combine(state, lax.dynamic_index_in_dim(gathered, source, 0, False))

    return lax.fori_loop(0, ahead, one, state)


def solve_block(state, basis_a, basis_b, denom):
    highest = lax.Precision.HIGHEST
    inner = lax.dot_general(
        basis_a,
        state,
        (((0,), (0,)), ((), ())),
        precision=highest,
        preferred_element_type=jnp.float32,
    )
    inner = jnp.dot(inner, basis_b, precision=highest, preferred_element_type=jnp.float32)
    inner = inner / denom
    outer = jnp.dot(basis_a, inner, precision=highest, preferred_element_type=jnp.float32)
    outer = lax.dot_general(
        outer,
        basis_b,
        (((1,), (1,)), ((), ())),
        precision=highest,
        preferred_element_type=jnp.float32,
    )
    return outer.astype(jnp.bfloat16)


def add_blocks(earlier, later):
    return earlier + later


def coupling_term(coup_a, coup_b, down, left, k_valid, m_valid):
    term_down = jnp.dot(coup_a, down, preferred_element_type=jnp.float32)
    term_left = jnp.dot(left, coup_b, preferred_element_type=jnp.float32)
    return jnp.where(k_valid, term_down, 0.0) + jnp.where(m_valid, term_left, 0.0)


def shards(rhs, a_coupling, b_coupling, a_basis, b_basis, a_vals, b_vals):
    rows_n = lax.axis_size("row")
    cols_n = lax.axis_size("col")
    row_at = lax.axis_index("row")
    col_at = lax.axis_index("col")
    first = (rows_n + cols_n) // 2 - 2
    level = rows_n - 1 - row_at + col_at
    denom = a_vals[:, None] + b_vals[None, :]
    state = rhs
    solution = jnp.zeros(rhs.shape, jnp.bfloat16)
    empty = jnp.zeros(rhs.shape, jnp.bfloat16)
    for step in range(3):
        active = level == first + step
        fresh = lax.cond(active, lambda: solve_block(state, a_basis, b_basis, denom), lambda: empty)
        solution = jnp.where(active, fresh, solution)
        k_index = col_at + rows_n - 1 - first - step
        m_index = row_at + first + step - rows_n + 1
        k_valid = (k_index > row_at) & (k_index < rows_n)
        m_valid = (m_index >= 0) & (m_index < col_at)
        down = carried_in(fresh, "row", add_blocks, empty, True)
        left = carried_in(fresh, "col", add_blocks, empty, False)
        state = state - coupling_term(
            a_coupling[step], b_coupling[step], down, left, k_valid, m_valid
        )
    rhs_next = jnp.where(level > first + 2, state, 0.0)
    return (solution, rhs_next)


def solution(mesh):
    placed = (
        P("row", "col"),
        P(None, "row", "col"),
        P(None, "row", "col"),
        P("row", None),
        P("col", None),
        P("row"),
        P("col"),
    )
    return jax.shard_map(
        shards,
        mesh=mesh,
        in_specs=placed,
        out_specs=(P("row", "col"), P("row", "col")),
        check_vma=False,
    )
```

profile of v0, /device:TPU:26, one launch (start us, length us, event | category | flops | bytes accessed | tf_op | source)
XLA Modules:
  0.0 250.3 jit_solution(16959247145825929377)
XLA Ops:
  10.4 1.3 copy.21
  11.7 35.6 %all-gather.7.cloned.1.call-done = bf16[4,384,384]{2,1,0:T(8,128)(2,1)} async-done(((bf16[1,384,384]{2,1,0:T(8,128)(2,1)}), bf16[4,384,384]{2,1,0:T(8,128)(2,1)}) %all-gather.7.cloned.1.call-update) | async-done | bytes 1179664 | tf_op jit(solution)/shard_map/all_gather | solution.py:11
  47.3 2.3 while.66
  49.6 2.2 fusion.9
  51.8 27.0 %all-gather.9.cloned.1.call-done = bf16[8,384,384]{2,1,0:T(8,128)(2,1)} async-done(((bf16[1,384,384]{2,1,0:T(8,128)(2,1)}), bf16[8,384,384]{2,1,0:T(8,128)(2,1)}) %all-gather.9.cloned.1.call-update) | async-done | bytes 2359312 | tf_op jit(solution)/shard_map/all_gather | solution.py:11
  78.8 6.8 %while.67 = (s32[]{:T(128)}, bf16[384,384]{1,0:T(8,128)(2,1)S(1)}, s32[]{:T(128)}, bf16[8,384,384]{2,1,0:T(8,128)(2,1)}, s32[]{:T(128)}, /*index=5*/s32[]{:T(128)}, s32[]{:T(128)}) while((s32[]{:T(128)}, bf16[384,384]{1,0:T(8,128)(2,1)S(1)}, s32[]{:T(128)}, bf16[8,384,384]{2,1,0:T(8,128)(2,1)}, s32[]{:T(128)}, /*index=5*/s32[]{:T(128)}, ...), condition=%wide.region_5.6_spmd, body=%wide.region_4.5_spmd.sunk | while | flops 147461 | bytes 884851 | solution.py:18
  78.8 1.2 bitcast_add_fusion.13
  81.2 1.1 bitcast_add_fusion.13
  85.6 1.6 fusion.8
  89.4 35.2 %all-gather.11.cloned.1.call-done = bf16[4,384,384]{2,1,0:T(8,128)(2,1)} async-done(((bf16[1,384,384]{2,1,0:T(8,128)(2,1)}), bf16[4,384,384]{2,1,0:T(8,128)(2,1)}) %all-gather.11.cloned.1.call-update) | async-done | bytes 1179664 | tf_op jit(solution)/shard_map/all_gather | solution.py:11
  124.6 2.3 while.68
  124.7 1.1 bitcast_add_fusion.14
  125.8 1.1 bitcast_add_fusion.14
  126.9 2.2 fusion.6
  129.1 26.8 %all-gather.13.cloned.1.call-done = bf16[8,384,384]{2,1,0:T(8,128)(2,1)} async-done(((bf16[1,384,384]{2,1,0:T(8,128)(2,1)}), bf16[8,384,384]{2,1,0:T(8,128)(2,1)}) %all-gather.13.cloned.1.call-update) | async-done | bytes 2359312 | tf_op jit(solution)/shard_map/all_gather | solution.py:11
  155.9 6.7 %while.69 = (s32[]{:T(128)}, bf16[384,384]{1,0:T(8,128)(2,1)S(1)}, s32[]{:T(128)}, bf16[8,384,384]{2,1,0:T(8,128)(2,1)}, s32[]{:T(128)}, /*index=5*/s32[]{:T(128)}, s32[]{:T(128)}) while((s32[]{:T(128)}, bf16[384,384]{1,0:T(8,128)(2,1)S(1)}, s32[]{:T(128)}, bf16[8,384,384]{2,1,0:T(8,128)(2,1)}, s32[]{:T(128)}, /*index=5*/s32[]{:T(128)}, ...), condition=%wide.region_11.12_spmd, body=%wide.region_10.11_spmd.sunk | while | flops 147461 | bytes 884851 | solution.py:18
  160.5 1.1 bitcast_add_fusion.15
  162.7 1.6 fusion.5
  167.2 35.8 %all-gather.15.cloned.1.call-done = bf16[4,384,384]{2,1,0:T(8,128)(2,1)} async-done(((bf16[1,384,384]{2,1,0:T(8,128)(2,1)}), bf16[4,384,384]{2,1,0:T(8,128)(2,1)}) %all-gather.15.cloned.1.call-update) | async-done | bytes 1179664 | tf_op jit(solution)/shard_map/all_gather | solution.py:11
  203.0 2.3 while.70
  205.3 1.4 fusion.3
  206.6 27.6 %all-gather.17.cloned.1.call-done = bf16[8,384,384]{2,1,0:T(8,128)(2,1)} async-done(((bf16[1,384,384]{2,1,0:T(8,128)(2,1)}), bf16[8,384,384]{2,1,0:T(8,128)(2,1)}) %all-gather.17.cloned.1.call-update) | async-done | bytes 2359312 | tf_op jit(solution)/shard_map/all_gather | solution.py:11
  234.3 6.7 %while.71 = (s32[]{:T(128)}, bf16[384,384]{1,0:T(8,128)(2,1)S(1)}, s32[]{:T(128)}, bf16[8,384,384]{2,1,0:T(8,128)(2,1)}, s32[]{:T(128)}, /*index=5*/s32[]{:T(128)}, s32[]{:T(128)}) while((s32[]{:T(128)}, bf16[384,384]{1,0:T(8,128)(2,1)S(1)}, s32[]{:T(128)}, bf16[8,384,384]{2,1,0:T(8,128)(2,1)}, s32[]{:T(128)}, /*index=5*/s32[]{:T(128)}, ...), condition=%wide.region_17.18_spmd, body=%wide.region_16.17_spmd.sunk | while | flops 147461 | bytes 884851 | solution.py:18
  241.1 1.4 fusion.2
  (59 shorter events, 32.5 us)
Async XLA Ops:
  7.2 40.1 %all-gather.7.cloned.1.call-start = ((), (), s32[]{:S(2)}) async-start(), calls=%async_computation | async-start | bytes 1474560 | tf_op jit(solution)/shard_map/all_gather | solution.py:11
  8.8 0.7 copy-start.4
  9.6 69.2 %all-gather.9.cloned.1.call-start = ((), (), s32[]{:S(2)}) async-start(), calls=%async_computation.1 | async-start | bytes 2654208 | tf_op jit(solution)/shard_map/all_gather | solution.py:11
  10.3 114.3 %all-gather.11.cloned.1.call-start = ((), (), s32[]{:S(2)}) async-start(), calls=%async_computation.2 | async-start | bytes 1474560 | tf_op jit(solution)/shard_map/all_gather | solution.py:11
  78.8 8.4 %copy-start = (f32[384,384]{1,0:T(8,128)S(1)}, f32[384,384]{1,0:T(8,128)}, u32[]{:S(2)}) copy-start(f32[384,384]{1,0:T(8,128)} %param.28) | copy-start | bytes 1769476
  78.8 8.4 %copy-start.2 = (f32[384,384]{1,0:T(8,128)S(1)}, f32[384,384]{1,0:T(8,128)}, u32[]{:S(2)}) copy-start(f32[384,384]{1,0:T(8,128)} %param.29) | copy-start | bytes 1769476
  88.0 0.7 copy-start.5
  88.7 67.2 %all-gather.13.cloned.1.call-start = ((), (), s32[]{:S(2)}) async-start(), calls=%async_computation.3 | async-start | bytes 2654208 | tf_op jit(solution)/shard_map/all_gather | solution.py:11
  89.3 113.6 %all-gather.15.cloned.1.call-start = ((), (), s32[]{:S(2)}) async-start(), calls=%async_computation.4 | async-start | bytes 1474560 | tf_op jit(solution)/shard_map/all_gather | solution.py:11
  165.1 0.7 copy-start.6
  165.8 68.5 %all-gather.17.cloned.1.call-start = ((), (), s32[]{:S(2)}) async-start(), calls=%async_computation.5 | async-start | bytes 2654208 | tf_op jit(solution)/shard_map/all_gather | solution.py:11
Sparse Core Ops, SparseCore 0:
  9.8 37.4 all-gather.6
  48.9 29.7 all-gather.8
  88.9 35.6 all-gather.10
  126.1 29.7 all-gather.12
  165.9 37.0 all-gather.14
  204.5 29.7 all-gather.16
where the time goes:
time: 253 us; the launch traced here: 250 us
  waiting for transfers between devices  190 us (75%)
  other arithmetic  28 us (11%)
  between operations  14.3 us (6%)
  matrix products  10.2 us (4%)
  local copies, waits for them, and re-layouts  6.93 us (3%)
    all_gather x6, waiting for transfers between devices, carried_in(): gathered = lax.all_gather(part, axis)  188 us
    add x24, other arithmetic, add_blocks(): return earlier + later  26.4 us
    dot_general x3, matrix products, coupling_term(): term_down = jnp.dot(coup_a, down, preferred_element_type=jnp.float32)  5.73 us
  transfers between devices with their start and end apart: 6, of which 6 were waited for; matrix products, arithmetic and copies ran while one was open for 6% of the time, Pallas kernels for 0%

commit v1 on v0

v1 whole, which is shorter than its diff:
```python
import functools

import jax
import jax.numpy as jnp
from jax import lax
from jax.experimental import pallas as pl
from jax.experimental.pallas import tpu as pltpu
from jax.sharding import PartitionSpec as P

AXES = ("row", "col")
VMEM_SPEC = pl.BlockSpec(memory_space=pltpu.VMEM)
ANY_SPEC = pl.BlockSpec(memory_space=pl.ANY)


def plan(rows_n, cols_n, offset, gap, up_gap):
    todo = []
    for i in range(rows_n):
        m = i + offset
        if 0 <= m < cols_n:
            targets = range(m + gap, cols_n)
            chips = sorted({j // 2 for j in targets}, reverse=True)
            for chip in chips:
                todo.append(("left", (i, m), [(i, j) for j in targets if j // 2 == chip]))
            if i - up_gap >= 0:
                todo.append(("down", (i, m), [(k, m) for k in range(i - up_gap, -1, -1)]))
    ops, forwards = [], []
    while todo or forwards:
        used_from, used_to, op, later = set(), set(), [], []

        def take(source, target, kind, forward):
            if source in used_from or target in used_to:
                return False
            used_from.add(source)
            used_to.add(target)
            op.append((source, target, kind, forward))
            return True

        kept = []
        for item in forwards:
            ready, source, target = item
            if not (ready <= len(ops) and take(source, target, "left", ready - 2)):
                kept.append(item)
        forwards = kept
        order = sorted(todo, key=lambda item: (item[0] == "down", len(item[2]) == 1))
        for item in order:
            kind, source, targets = item
            if kind == "left":
                for target in targets:
                    if take(source, target, kind, None):
                        todo.remove(item)
                        rest = [other for other in targets if other != target]
                        later += [(len(ops) + 2, target, other) for other in rest]
                        break
            else:
                for target in targets:
                    if take(source, target, kind, None):
                        targets.remove(target)
                        break
                if not targets:
                    todo.remove(item)
        forwards += later
        ops.append(op)
    return ops


def one_of(me, ids):
    hit = me < 0
    for each in sorted(ids):
        hit = hit | (me == each)
    return hit


def place(cols_n):
    return lax.axis_index("row") * cols_n + lax.axis_index("col")


def level_of(rows_n):
    return rows_n - 1 - lax.axis_index("row") + lax.axis_index("col")


def dot(a, b):
    return lax.dot_general(a, b, (((1,), (0,)), ((), ())), preferred_element_type=jnp.float32)


def split(x):
    high = x.astype(jnp.bfloat16)
    return high, (x - high.astype(jnp.float32)).astype(jnp.bfloat16)


def put_left(ref, pair):
    n = pair[0].shape[1]
    ref[:, 0:n] = pair[0]
    ref[:, n : 2 * n] = pair[0]
    ref[:, 2 * n : 3 * n] = pair[1]


def put_right(ref, pair):
    n = pair[0].shape[0]
    ref[0:n] = pair[0]
    ref[n : 2 * n] = pair[1]
    ref[2 * n : 3 * n] = pair[0]


def solve(state, uk, utk, vk, vtk, inverse, lhs, rhs):
    put_left(lhs, split(state))
    part = dot(lhs[...], vk[...])
    put_right(rhs, split(part))
    part = dot(utk[...], rhs[...]) * inverse[...]
    put_left(lhs, split(part))
    part = dot(lhs[...], vtk[...])
    put_right(rhs, split(part))
    return dot(uk[...], rhs[...]).astype(jnp.bfloat16)


def copies(pairs, sem):
    moves = [pltpu.make_async_copy(source, target, sem.at[n]) for n, (source, target) in enumerate(pairs)]
    for move in moves:
        move.start()
    return moves


def begin(rows_n, first, rhs, a_c, b_c, u_any, v_any, av, bv, f0, uk, utk, vk, vtk, inverse, s, ca, cb, u, v, lhs, mid, sem):
    level = level_of(rows_n)

    @pl.when((level >= first) & (level <= first + 2))
    def _():
        moves = copies(((u_any, u), (v_any, v), (rhs, s), (a_c.at[0], ca), (b_c.at[0], cb)), sem)
        n = u.shape[0]
        alpha = jnp.transpose(jnp.broadcast_to(av[...], (128, n)))
        for c in range(0, n, 128):
            inverse[:, c : c + 128] = 1.0 / (alpha + bv[:, c : c + 128])
        moves[0].wait()
        high, low = split(u[...])
        put_left(uk, (high, low))
        put_left(utk, (high.T, low.T))
        moves[1].wait()
        high, low = split(v[...])
        put_right(vk, (high, low))
        put_right(vtk, (high.T, low.T))
        moves[2].wait()
        moves[3].wait()
        moves[4].wait()

    @pl.when(level == first)
    def _():
        f0[...] = solve(s[...], uk, utk, vk, vtk, inverse, lhs, mid)


def second(rows_n, first, down, left, uk, utk, vk, vtk, inverse, s, ca, cb, f1, pair_l, pair_d, lhs, mid):
    @pl.when(level_of(rows_n) == first + 1)
    def _():
        n = s.shape[0]
        state = s[...] - (dot(ca[...], down[...]) + dot(left[...], cb[...]))
        block = solve(state, uk, utk, vk, vtk, inverse, lhs, mid)
        f1[...] = block
        pair_l[0:n] = left[...]
        pair_l[n:] = block
        pair_d[0:n] = down[...]
        pair_d[n:] = block


def third_early(rows_n, first, a_c, b_c, down, left, s, ca, cb, s1, a1, b1, sem):
    @pl.when(level_of(rows_n) == first + 2)
    def _():
        moves = copies(((a_c.at[1], a1), (b_c.at[1], b1)), sem)
        s1[...] = s[...] - (dot(ca[...], down[...]) + dot(left[...], cb[...]))
        for move in moves:
            move.wait()


def third(rows_n, cols_n, first, ops, rhs, a_c, b_c, down, left, uk, utk, vk, vtk, inverse, s1, a1, b1, *rest):
    arrived, (f2, s2, a2, b2, lhs, mid, av, bv, got, sem) = rest[: len(ops)], rest[len(ops) :]
    level = level_of(rows_n)

    @pl.when(level == first + 2)
    def _():
        state = s1[...] - (dot(a1[...], down[...]) + dot(left[...], b1[...]))
        f2[...] = solve(state, uk, utk, vk, vtk, inverse, lhs, mid)

    @pl.when(level > first + 2)
    def _():
        n = s2.shape[0]
        moves = copies(((rhs, s2), (a_c.at[0:2], av), (b_c.at[0:2], bv), (a_c.at[2], a2), (b_c.at[2], b2)), sem)
        for move in moves:
            move.wait()
        for kind in ("left", "down"):
            hits = pick(cols_n, ops, kind, arrived, got)

            @pl.when(hits)
            def _():
                for t in range(2):
                    block = got[t * n : (t + 1) * n]
                    s2[...] -= dot(block, bv[t]) if kind == "left" else dot(av[t], block)


def pick(cols_n, ops, kind, arrived, got):
    me = place(cols_n)
    any_hit = me < 0
    for op, ref in zip(ops, arrived):
        hit = one_of(me, [t[0] * cols_n + t[1] for _, t, k, _ in op if k == kind])
        any_hit = any_hit | hit

        @pl.when(hit)
        def _():
            got[...] = ref[...]

    return any_hit


def finish(rows_n, cols_n, first, ops, f0, f1, f2, s2, a2, b2, *rest):
    arrived, (out, nxt, got) = rest[: len(ops)], rest[len(ops) :]
    level = level_of(rows_n)
    out[...] = jnp.zeros(out.shape, out.dtype)
    for t, block in enumerate((f0, f1, f2)):

        @pl.when(level == first + t)
        def _():
            out[...] = block[...]

    @pl.when(level <= first + 2)
    def _():
        nxt[...] = jnp.zeros(nxt.shape, nxt.dtype)

    @pl.when(level > first + 2)
    def _():
        nxt[...] = s2[...]
        for kind in ("down", "left"):
            hits = pick(cols_n, ops, kind, arrived, got)

            @pl.when(hits)
            def _():
                nxt[...] -= dot(got[...], b2[...]) if kind == "left" else dot(a2[...], got[...])


def spread(ops, cols_n, own):
    me = place(cols_n)
    arrived = []
    for op in ops:
        value = own["left"]
        if own["down"] is not own["left"]:
            downs = [s[0] * cols_n + s[1] for s, _, k, _ in op if k == "down"]
            if downs:
                value = jnp.where(one_of(me, downs), own["down"], value)
        for earlier in sorted({f for *_, f in op if f is not None}):
            ids = [s[0] * cols_n + s[1] for s, _, _, f in op if f == earlier]
            value = jnp.where(one_of(me, ids), arrived[earlier], value)
        pairs = [(s[0] * cols_n + s[1], t[0] * cols_n + t[1]) for s, t, _, _ in op]
        arrived.append(lax.ppermute(value, AXES, pairs))
    return arrived


def solution(mesh):
    rows_n, cols_n = mesh.shape["row"], mesh.shape["col"]
    first = (rows_n + cols_n) // 2 - 2
    offset = first - rows_n + 1
    pair_ops = plan(rows_n, cols_n, offset + 1, 2, 2)
    last_ops = plan(rows_n, cols_n, offset + 2, 1, 1)

    def owners(t):
        return [(i, i + offset + t) for i in range(rows_n) if 0 <= i + offset + t < cols_n]

    def up(t, far):
        return [(i * cols_n + j, (i - far) * cols_n + j) for i, j in owners(t) if i >= far]

    def right(t, far):
        return [(i * cols_n + j, i * cols_n + j + far) for i, j in owners(t) if j + far < cols_n]

    def shards(rhs, a_c, b_c, u, v, a_vals, b_vals):
        n = rhs.shape[0]
        half, full = jnp.bfloat16, jnp.float32
        square = jax.ShapeDtypeStruct((n, n), half)
        wide, tall = jax.ShapeDtypeStruct((n, 3 * n), half), jax.ShapeDtypeStruct((3 * n, n), half)
        pair = jax.ShapeDtypeStruct((2 * n, n), half)
        state = jax.ShapeDtypeStruct((n, n), full)
        work = [pltpu.VMEM((n, 3 * n), half), pltpu.VMEM((3 * n, n), half)]

        def call(kernel, ins, outs, scratch, name):
            return pl.pallas_call(
                kernel,
                out_shape=outs,
                in_specs=[ANY_SPEC if far else VMEM_SPEC for _, far in ins],
                out_specs=[VMEM_SPEC] * len(outs),
                scratch_shapes=scratch,
                compiler_params=pltpu.CompilerParams(vmem_limit_bytes=24 << 20),
                name=name,
            )(*[x for x, _ in ins])

        def hbm(*xs):
            return [(x, True) for x in xs]

        def near(*xs):
            return [(x, False) for x in xs]

        f0, uk, utk, vk, vtk, inverse, s, ca, cb = call(
            functools.partial(begin, rows_n, first),
            hbm(rhs, a_c, b_c, u, v) + near(a_vals.reshape(1, n), b_vals.reshape(1, n)),
            [square, wide, wide, tall, tall, state, state, square, square],
            [pltpu.VMEM((n, n), full)] * 2 + work + [pltpu.SemaphoreType.DMA((5,))],
            "begin",
        )
        basis = near(uk, utk, vk, vtk, inverse)
        down = lax.ppermute(f0, AXES, up(0, 1))
        left = lax.ppermute(f0, AXES, right(0, 1))
        down_far = lax.ppermute(f0, AXES, up(0, 2))
        left_far = lax.ppermute(f0, AXES, right(0, 2))
        f1, pair_l, pair_d = call(
            functools.partial(second, rows_n, first),
            near(down, left) + basis + near(s, ca, cb),
            [square, pair, pair],
            work,
            "second",
        )
        down = lax.ppermute(f1, AXES, up(1, 1))
        left = lax.ppermute(f1, AXES, right(1, 1))
        s1, a1, b1 = call(
            functools.partial(third_early, rows_n, first),
            hbm(a_c, b_c) + near(down_far, left_far, s, ca, cb),
            [state, square, square],
            [pltpu.SemaphoreType.DMA((2,))],
            "third_early",
        )
        pairs = spread(pair_ops, cols_n, {"left": pair_l, "down": pair_d})
        f2, s2, a2, b2 = call(
            functools.partial(third, rows_n, cols_n, first, pair_ops),
            hbm(rhs, a_c, b_c) + near(down, left) + basis + near(s1, a1, b1, *pairs),
            [square, state, square, square],
            work
            + [pltpu.VMEM((2, n, n), half)] * 2
            + [pltpu.VMEM((2 * n, n), half), pltpu.SemaphoreType.DMA((5,))],
            "third",
        )
        lasts = spread(last_ops, cols_n, {"left": f2, "down": f2})
        return call(
            functools.partial(finish, rows_n, cols_n, first, last_ops),
            near(f0, f1, f2, s2, a2, b2, *lasts),
            [square, state],
            [pltpu.VMEM((n, n), half)],
            "finish",
        )

    placed = (
        P("row", "col"),
        P(None, "row", "col"),
        P(None, "row", "col"),
        P("row", None),
        P("col", None),
        P("row"),
        P("col"),
    )
    return jax.shard_map(
        shards,
        mesh=mesh,
        in_specs=placed,
        out_specs=(P("row", "col"), P("row", "col")),
        check_vma=False,
    )
```

time: 253 us -> 84.3 us (0.33)
  waiting for transfers between devices: 190 us -> 45.7 us
  other arithmetic: 28 us -> 3.76 us
  starting transfers between devices: 0.24 us -> 14.4 us
  between operations: 14.3 us -> 0.97 us
  matrix products: 10.2 us -> 0 us
  Pallas kernels: 0 us -> 7.81 us
  local copies, waits for them, and re-layouts: 6.93 us -> 10.9 us
    all_gather x6 -> x0, waiting for transfers between devices: 188 us -> none  [carried_in(): gathered = lax.all_gather(part, axis)]
    ppermute x0 -> x14, waiting for transfers between devices: none -> 45.7 us  [the longest x8 45.6 us: spread(): arrived.append(lax.ppermute(value, AXES, pairs))]
    add x25 -> x0, other arithmetic: 27.2 us -> none  [the longest x24 26.4 us: add_blocks(): return earlier + later]
    ppermute x0 -> x14, starting transfers between devices: none -> 14.4 us  [the longest x8 9.59 us: spread(): arrived.append(lax.ppermute(value, AXES, pairs))]
    dot_general x6 -> x0, matrix products: 10.2 us -> none  [the longest x3 5.73 us: coupling_term(): term_down = jnp.dot(coup_a, down, preferred_element_type=jnp.float32)]
    pallas_call x0 -> x5, Pallas kernels: none -> 7.81 us  [call(): pl.pallas_call(kernel, out_shape=outs, in_specs=[ANY_SPEC if far else VME...]
    unnamed x12 -> x40, local copies, waits for them, and re-layouts: 4.45 us -> 10.2 us
    select_n x1 -> x3, other arithmetic: 0.79 us -> 3.76 us  [spread(): value = jnp.where(one_of(me, ids), arrived[earlier], value)]
  transfers between devices with their start and end apart: 6 -> 14, of which waited for: 6 -> 3; matrix products, arithmetic and copies ran while one was open for 6% -> 1% of each run, Pallas kernels for 0% -> 1%
where the time goes in v1:
time: 84.3 us; the launch traced here: 83.5 us
  waiting for transfers between devices  45.7 us (54%)
  starting transfers between devices  14.4 us (17%)
  local copies, waits for them, and re-layouts  10.9 us (13%)
  Pallas kernels  7.81 us (9%)
  other arithmetic  3.76 us (4%)
  between operations  0.97 us (1%)
    ppermute x8, waiting for transfers between devices, spread(): arrived.append(lax.ppermute(value, AXES, pairs))  45.6 us
    unnamed x40, local copies, waits for them, and re-layouts  10.2 us
    ppermute x8, starting transfers between devices, spread(): arrived.append(lax.ppermute(value, AXES, pairs))  9.59 us
    pallas_call x5, Pallas kernels, call(): pl.pallas_call(kernel, out_shape=outs, in_specs=[ANY_SPEC if far else VME...  7.81 us
    select_n x3, other arithmetic, spread(): value = jnp.where(one_of(me, ids), arrived[earlier], value)  3.76 us
  transfers between devices with their start and end apart: 14, of which 3 were waited for; matrix products, arithmetic and copies ran while one was open for 1% of the time, Pallas kernels for 1%

profile of v1, /device:TPU:26, one launch (start us, length us, event | category | flops | bytes accessed | tf_op | source)
XLA Modules:
  0.0 83.5 jit_solution(1055967639903449538)
XLA Ops:
  1.3 1.2 %copy-done = bf16[3,384,384]{2,1,0:T(8,128)(2,1)S(1)} copy-done((bf16[3,384,384]{2,1,0:T(8,128)(2,1)S(1)}, bf16[3,384,384]{2,1,0:T(8,128)(2,1)}, u32[]{:S(2)}) %copy-start) | copy-done | bytes 884760
  2.5 1.2 %copy-done.2 = bf16[3,384,384]{2,1,0:T(8,128)(2,1)S(1)} copy-done((bf16[3,384,384]{2,1,0:T(8,128)(2,1)S(1)}, bf16[3,384,384]{2,1,0:T(8,128)(2,1)}, u32[]{:S(2)}) %copy-start.2) | copy-done | bytes 884760
  3.7 1.1 %copy-done.8 = f32[384,384]{1,0:T(8,128)S(1)} copy-done((f32[384,384]{1,0:T(8,128)S(1)}, f32[384,384]{1,0:T(8,128)}, u32[]{:S(2)}) %copy-start.8) | copy-done | bytes 589848
  4.7 1.1 %copy-done.14 = f32[384,384]{1,0:T(8,128)S(1)} copy-done((f32[384,384]{1,0:T(8,128)S(1)}, f32[384,384]{1,0:T(8,128)}, u32[]{:S(2)}) %copy-start.14) | copy-done | bytes 589848
  5.8 1.1 %copy-done.15 = f32[384,384]{1,0:T(8,128)S(1)} copy-done((f32[384,384]{1,0:T(8,128)S(1)}, f32[384,384]{1,0:T(8,128)}, u32[]{:S(2)}) %copy-start.15) | copy-done | bytes 589848
  9.1 0.8 second.1
  11.4 1.3 %collective-permute-start.6 = (bf16[768,384]{1,0:T(8,128)(2,1)}, bf16[768,384]{1,0:T(8,128)(2,1)}, u32[]{:S(2)}, u32[]{:S(2)}) collective-permute-start(bf16[768,384]{1,0:T(8,128)(2,1)} %get-tuple-element.34), channel_id=1, source_target_pairs={{2,6},{11,14},{20,22},{29,31}} | collective-permute-start | bytes 1769480 | tf_op jit(solution)/shard_map/ppermute | solution.py:248
  12.7 24.1 %collective-permute-done.6.rest_0_ = bf16[768,384]{1,0:T(8,128)(2,1)} collective-permute-done((bf16[768,384]{1,0:T(8,128)(2,1)}, bf16[768,384]{1,0:T(8,128)(2,1)}, u32[]{:S(2)}, u32[]{:S(2)}) %collective-permute-start.6) | collective-permute-done | bytes 589856 | tf_op jit(solution)/shard_map/ppermute | solution.py:248
  36.8 2.5 %select_select_fusion = (bf16[768,384]{1,0:T(8,128)(2,1)}, bf16[768,384]{1,0:T(8,128)(2,1)}) fusion(bf16[768,384]{1,0:T(8,128)(2,1)} %collective-permute-done.6.rest_0_, bf16[768,384]{1,0:T(8,128)(2,1)} %copy-done.16, bf16[768,384]{1,0:T(8,128)(2,1)} %get-tuple-element.34, pred[]{:T(512)S(6)} %or.30, pred[]{:T(512)S(6)} %or.28, pred[]{:T(512)S(6)} %or.25), kind=kLoop, calls=%fused_computation | loop fusion | flops 884736 | bytes 2949123 | tf_op jit(solution)/shard_map/jit(_where)/select_n | solution.py:246
  39.4 1.5 %collective-permute-start.7 = (bf16[768,384]{1,0:T(8,128)(2,1)}, bf16[768,384]{1,0:T(8,128)(2,1)}, u32[]{:S(2)}, u32[]{:S(2)}) collective-permute-start(bf16[768,384]{1,0:T(8,128)(2,1)} %get-tuple-element.41), channel_id=1, source_target_pairs={{2,4},{11,13},{29,5}} | collective-permute-start | bytes 1769480 | tf_op jit(solution)/shard_map/ppermute | solution.py:248
  40.8 1.4 %collective-permute-start.5 = (bf16[384,384]{1,0:T(8,128)(2,1)}, bf16[384,384]{1,0:T(8,128)(2,1)}, u32[]{:S(2)}, u32[]{:S(2)}) collective-permute-start(bf16[384,384]{1,0:T(8,128)(2,1)} %get-tuple-element.21.f0), channel_id=1, source_target_pairs={{1,3},{10,12},{19,21},{28,30}} | collective-permute-start | bytes 884744 | tf_op jit(solution)/shard_map/ppermute | solution.py:305
  42.2 1.4 %collective-permute-start.8 = (bf16[768,384]{1,0:T(8,128)(2,1)}, bf16[768,384]{1,0:T(8,128)(2,1)S(1)}, u32[]{:S(2)}, u32[]{:S(2)}) collective-permute-start(bf16[768,384]{1,0:T(8,128)(2,1)} %get-tuple-element.40), channel_id=1, source_target_pairs={{6,7},{14,15},{22,23},{20,4},{29,13}} | collective-permute-start | bytes 1769480 | tf_op jit(solution)/shard_map/ppermute | solution.py:248
  43.7 1.2 %broadcast_select_fusion = bf16[768,384]{1,0:T(8,128)(2,1)S(1)} fusion(bf16[768,384]{1,0:T(8,128)(2,1)} %collective-permute-done.7.rest_1_, bf16[768,384]{1,0:T(8,128)(2,1)} %get-tuple-element.34, pred[]{:T(512)S(6)} %or.31), kind=kLoop, calls=%fused_computation.1 | loop fusion | flops 294912 | bytes 1769473 | tf_op jit(solution)/shard_map/jit(_where)/select_n | solution.py:246
  47.6 1.1 %copy-done.5 = f32[384,384]{1,0:T(8,128)S(1)} copy-done((f32[384,384]{1,0:T(8,128)S(1)}, f32[384,384]{1,0:T(8,128)}, u32[]{:S(2)}) %copy-start.5) | copy-done | bytes 589848
  48.7 1.0 %copy-done.11 = bf16[384,384]{1,0:T(8,128)(2,1)S(1)} copy-done((bf16[384,384]{1,0:T(8,128)(2,1)S(1)}, bf16[384,384]{1,0:T(8,128)(2,1)}, u32[]{:S(2)}) %copy-start.11) | copy-done | bytes 294936
  49.7 1.0 %copy-done.13 = bf16[384,384]{1,0:T(8,128)(2,1)S(1)} copy-done((bf16[384,384]{1,0:T(8,128)(2,1)S(1)}, bf16[384,384]{1,0:T(8,128)(2,1)}, u32[]{:S(2)}) %copy-start.13) | copy-done | bytes 294936
  50.6 1.1 %third_early.1 = (f32[384,384]{1,0:T(8,128)S(1)}, bf16[384,384]{1,0:T(8,128)(2,1)S(1)}, bf16[384,384]{1,0:T(8,128)(2,1)S(1)}) custom-call(bf16[3,384,384]{2,1,0:T(8,128)(2,1)S(1)} %copy-done.1, bf16[3,384,384]{2,1,0:T(8,128)(2,1)S(1)} %copy-done.3, bf16[384,384]{1,0:T(8,128)(2,1)S(1)} %collective-permute-done.4.down, ...), custom_call_target="tpu_custom_call" | custom-call | tf_op jit(solution)/shard_map/third_early/pallas_call | solution.py:278
  52.0 2.5 %third.1 = (bf16[384,384]{1,0:T(8,128)(2,1)S(1)}, f32[384,384]{1,0:T(8,128)S(1)}, bf16[384,384]{1,0:T(8,128)(2,1)S(1)}, bf16[384,384]{1,0:T(8,128)(2,1)S(1)}) custom-call(f32[384,384]{1,0:T(8,128)S(1)} %copy-done.9, bf16[3,384,384]{2,1,0:T(8,128)(2,1)S(1)} %copy-done.1, bf16[3,384,384]{2,1,0:T(8,128)(2,1)S(1)} %copy-done.3, ...), custom_call_target="tpu_custom_call" | custom-call | tf_op jit(solution)/shard_map/third/pallas_call | solution.py:278
  54.4 0.8 collective-permute-start.11
  55.2 1.3 %collective-permute-start.10 = (bf16[384,384]{1,0:T(8,128)(2,1)S(1)}, bf16[384,384]{1,0:T(8,128)(2,1)S(1)}, u32[]{:S(2)}, u32[]{:S(2)}) collective-permute-start(bf16[384,384]{1,0:T(8,128)(2,1)S(1)} %get-tuple-element.36.f2), channel_id=1, source_target_pairs={{3,6},{12,14},{21,22},{30,31}} | collective-permute-start | bytes 884744 | tf_op jit(solution)/shard_map/ppermute | solution.py:248
  56.6 11.0 %collective-permute-done.10.rest_0_ = bf16[384,384]{1,0:T(8,128)(2,1)S(1)} collective-permute-done((bf16[384,384]{1,0:T(8,128)(2,1)S(1)}, bf16[384,384]{1,0:T(8,128)(2,1)S(1)}, u32[]{:S(2)}, u32[]{:S(2)}) %collective-permute-start.10) | collective-permute-done | bytes 294944 | tf_op jit(solution)/shard_map/ppermute | solution.py:248
  68.3 1.9 %collective-permute-start.12 = (bf16[384,384]{1,0:T(8,128)(2,1)S(1)}, bf16[384,384]{1,0:T(8,128)(2,1)S(1)}, u32[]{:S(2)}, u32[]{:S(2)}) collective-permute-start(bf16[384,384]{1,0:T(8,128)(2,1)S(1)} %get-tuple-element.43), channel_id=1, source_target_pairs={{6,7},{14,15},{22,23},{30,14},{12,4},{21,13}} | collective-permute-start | bytes 884744 | tf_op jit(solution)/shard_map/ppermute | solution.py:248
  70.3 10.5 %collective-permute-done.12.rest_2_ = bf16[384,384]{1,0:T(8,128)(2,1)S(1)} collective-permute-done((bf16[384,384]{1,0:T(8,128)(2,1)S(1)}, bf16[384,384]{1,0:T(8,128)(2,1)S(1)}, u32[]{:S(2)}, u32[]{:S(2)}) %collective-permute-start.12) | collective-permute-done | bytes 294944 | tf_op jit(solution)/shard_map/ppermute | solution.py:248
  80.8 2.7 %finish.1 = (bf16[384,384]{1,0:T(8,128)(2,1)}, f32[384,384]{1,0:T(8,128)}) custom-call(bf16[384,384]{1,0:T(8,128)(2,1)} %get-tuple-element.21.f0, bf16[384,384]{1,0:T(8,128)(2,1)S(1)} %copy-done.18, bf16[384,384]{1,0:T(8,128)(2,1)S(1)} %get-tuple-element.36.f2, f32[384,384]{1,0:T(8,128)S(1)} %get-tuple-element.37.s2, ...), custom_call_target="tpu_custom_call" | custom-call | tf_op jit(solution)/shard_map/finish/pallas_call | solution.py:278
  (54 shorter events, 8.1 us)
Async XLA Ops:
  1.3 1.2 %copy-start = (bf16[3,384,384]{2,1,0:T(8,128)(2,1)S(1)}, bf16[3,384,384]{2,1,0:T(8,128)(2,1)}, u32[]{:S(2)}) copy-start(bf16[3,384,384]{2,1,0:T(8,128)(2,1)} %a_c.5) | copy-start | bytes 2654212
  2.5 1.2 %copy-start.2 = (bf16[3,384,384]{2,1,0:T(8,128)(2,1)S(1)}, bf16[3,384,384]{2,1,0:T(8,128)(2,1)}, u32[]{:S(2)}) copy-start(bf16[3,384,384]{2,1,0:T(8,128)(2,1)} %b_c.5) | copy-start | bytes 2654212
  7.6 2.3 %copy-start.4 = (f32[384,384]{1,0:T(8,128)}, f32[384,384]{1,0:T(8,128)S(1)}, u32[]{:S(2)}) copy-start(f32[384,384]{1,0:T(8,128)S(1)} %get-tuple-element.27.s) | copy-start | bytes 1769476
  7.6 2.3 %copy-start.6 = (f32[384,384]{1,0:T(8,128)}, f32[384,384]{1,0:T(8,128)S(1)}, u32[]{:S(2)}) copy-start(f32[384,384]{1,0:T(8,128)S(1)} %get-tuple-element.26.inverse) | copy-start | bytes 1769476
  7.6 2.3 %copy-start.10 = (bf16[384,384]{1,0:T(8,128)(2,1)}, bf16[384,384]{1,0:T(8,128)(2,1)S(1)}, u32[]{:S(2)}) copy-start(bf16[384,384]{1,0:T(8,128)(2,1)S(1)} %get-tuple-element.28.ca) | copy-start | bytes 884740
  7.7 2.3 %copy-start.12 = (bf16[384,384]{1,0:T(8,128)(2,1)}, bf16[384,384]{1,0:T(8,128)(2,1)S(1)}, u32[]{:S(2)}) copy-start(bf16[384,384]{1,0:T(8,128)(2,1)S(1)} %get-tuple-element.29.cb) | copy-start | bytes 884740
  7.7 1.4 %collective-permute-start.1 = (bf16[384,384]{1,0:T(8,128)(2,1)}, bf16[384,384]{1,0:T(8,128)(2,1)S(1)}, u32[]{:S(2)}, u32[]{:S(2)}) collective-permute-start(bf16[384,384]{1,0:T(8,128)(2,1)} %get-tuple-element.21.f0), channel_id=1, source_target_pairs={{1,2},{10,11},{19,20},{28,29}} | collective-permute-start | bytes 884744 | tf_op jit(solution)/shard_map/ppermute | solution.py:303
  8.3 0.7 collective-permute-start
  11.4 25.4 %collective-permute-start.6 = (bf16[768,384]{1,0:T(8,128)(2,1)}, bf16[768,384]{1,0:T(8,128)(2,1)}, u32[]{:S(2)}, u32[]{:S(2)}) collective-permute-start(bf16[768,384]{1,0:T(8,128)(2,1)} %get-tuple-element.34), channel_id=1, source_target_pairs={{2,6},{11,14},{20,22},{29,31}} | collective-permute-start | bytes 1769480 | tf_op jit(solution)/shard_map/ppermute | solution.py:248
  39.4 4.3 %collective-permute-start.7 = (bf16[768,384]{1,0:T(8,128)(2,1)}, bf16[768,384]{1,0:T(8,128)(2,1)}, u32[]{:S(2)}, u32[]{:S(2)}) collective-permute-start(bf16[768,384]{1,0:T(8,128)(2,1)} %get-tuple-element.41), channel_id=1, source_target_pairs={{2,4},{11,13},{29,5}} | collective-permute-start | bytes 1769480 | tf_op jit(solution)/shard_map/ppermute | solution.py:248
  40.8 6.1 %collective-permute-start.5 = (bf16[384,384]{1,0:T(8,128)(2,1)}, bf16[384,384]{1,0:T(8,128)(2,1)}, u32[]{:S(2)}, u32[]{:S(2)}) collective-permute-start(bf16[384,384]{1,0:T(8,128)(2,1)} %get-tuple-element.21.f0), channel_id=1, source_target_pairs={{1,3},{10,12},{19,21},{28,30}} | collective-permute-start | bytes 884744 | tf_op jit(solution)/shard_map/ppermute | solution.py:305
  42.2 5.4 %copy-start.1 = (bf16[3,384,384]{2,1,0:T(8,128)(2,1)S(1)}, bf16[3,384,384]{2,1,0:T(8,128)(2,1)}, u32[]{:S(2)}) copy-start(bf16[3,384,384]{2,1,0:T(8,128)(2,1)} %a_c.5) | copy-start | bytes 2654212
  42.2 5.4 %copy-start.3 = (bf16[3,384,384]{2,1,0:T(8,128)(2,1)S(1)}, bf16[3,384,384]{2,1,0:T(8,128)(2,1)}, u32[]{:S(2)}) copy-start(bf16[3,384,384]{2,1,0:T(8,128)(2,1)} %b_c.5) | copy-start | bytes 2654212
  42.2 9.5 %collective-permute-start.8 = (bf16[768,384]{1,0:T(8,128)(2,1)}, bf16[768,384]{1,0:T(8,128)(2,1)S(1)}, u32[]{:S(2)}, u32[]{:S(2)}) collective-permute-start(bf16[768,384]{1,0:T(8,128)(2,1)} %get-tuple-element.40), channel_id=1, source_target_pairs={{6,7},{14,15},{22,23},{20,4},{29,13}} | collective-permute-start | bytes 1769480 | tf_op jit(solution)/shard_map/ppermute | solution.py:248
  44.8 6.9 %collective-permute-start.9 = (bf16[768,384]{1,0:T(8,128)(2,1)S(1)}, bf16[768,384]{1,0:T(8,128)(2,1)S(1)}, u32[]{:S(2)}, u32[]{:S(2)}) collective-permute-start(bf16[768,384]{1,0:T(8,128)(2,1)S(1)} %broadcast_select_fusion), channel_id=1, source_target_pairs={{4,5}} | collective-permute-start | bytes 1769480 | tf_op jit(solution)/shard_map/ppermute | solution.py:248
  45.5 2.1 %collective-permute-start.4 = (bf16[384,384]{1,0:T(8,128)(2,1)}, bf16[384,384]{1,0:T(8,128)(2,1)S(1)}, u32[]{:S(2)}, u32[]{:S(2)}) collective-permute-start(bf16[384,384]{1,0:T(8,128)(2,1)} %get-tuple-element.21.f0), channel_id=1, source_target_pairs={{19,3},{28,12}} | collective-permute-start | bytes 884744 | tf_op jit(solution)/shard_map/ppermute | solution.py:304
  46.2 5.5 %collective-permute-start.3 = (bf16[384,384]{1,0:T(8,128)(2,1)}, bf16[384,384]{1,0:T(8,128)(2,1)S(1)}, u32[]{:S(2)}, u32[]{:S(2)}) collective-permute-start(bf16[384,384]{1,0:T(8,128)(2,1)} %copy-done.17), channel_id=1, source_target_pairs={{2,3},{11,12},{20,21},{29,30}} | collective-permute-start | bytes 884744 | tf_op jit(solution)/shard_map/ppermute | solution.py:314
  46.9 4.8 %collective-permute-start.2 = (bf16[384,384]{1,0:T(8,128)(2,1)}, bf16[384,384]{1,0:T(8,128)(2,1)S(1)}, u32[]{:S(2)}, u32[]{:S(2)}) collective-permute-start(bf16[384,384]{1,0:T(8,128)(2,1)} %copy-done.17), channel_id=1, source_target_pairs={{11,3},{20,12},{29,21}} | collective-permute-start | bytes 884744 | tf_op jit(solution)/shard_map/ppermute | solution.py:313
  50.6 1.3 %copy-start.9 = (f32[384,384]{1,0:T(8,128)S(1)}, f32[384,384]{1,0:T(8,128)}, u32[]{:S(2)}) copy-start(f32[384,384]{1,0:T(8,128)} %rhs.3) | copy-start | bytes 1769476
  54.4 26.4 %copy-start.18 = (bf16[384,384]{1,0:T(8,128)(2,1)S(1)}, bf16[384,384]{1,0:T(8,128)(2,1)}, u32[]{:S(2)}) copy-start(bf16[384,384]{1,0:T(8,128)(2,1)} %copy-done.17) | copy-start | bytes 884740
  54.4 2.1 %collective-permute-start.11 = (bf16[384,384]{1,0:T(8,128)(2,1)S(1)}, bf16[384,384]{1,0:T(8,128)(2,1)S(1)}, u32[]{:S(2)}, u32[]{:S(2)}) collective-permute-start(bf16[384,384]{1,0:T(8,128)(2,1)S(1)} %get-tuple-element.36.f2), channel_id=1, source_target_pairs={{3,4},{12,13},{21,5},{30,22}} | collective-permute-start | bytes 884744 | tf_op jit(solution)/shard_map/ppermute | solution.py:248
  55.2 12.3 %collective-permute-start.10 = (bf16[384,384]{1,0:T(8,128)(2,1)S(1)}, bf16[384,384]{1,0:T(8,128)(2,1)S(1)}, u32[]{:S(2)}, u32[]{:S(2)}) collective-permute-start(bf16[384,384]{1,0:T(8,128)(2,1)S(1)} %get-tuple-element.36.f2), channel_id=1, source_target_pairs={{3,6},{12,14},{21,22},{30,31}} | collective-permute-start | bytes 884744 | tf_op jit(solution)/shard_map/ppermute | solution.py:248
  67.7 2.6 %collective-permute-start.13 = (bf16[384,384]{1,0:T(8,128)(2,1)S(1)}, bf16[384,384]{1,0:T(8,128)(2,1)S(1)}, u32[]{:S(2)}, u32[]{:S(2)}) collective-permute-start(bf16[384,384]{1,0:T(8,128)(2,1)S(1)} %get-tuple-element.42), channel_id=1, source_target_pairs={{4,5},{30,6}} | collective-permute-start | bytes 884744 | tf_op jit(solution)/shard_map/ppermute | solution.py:248
  68.3 12.4 %collective-permute-start.12 = (bf16[384,384]{1,0:T(8,128)(2,1)S(1)}, bf16[384,384]{1,0:T(8,128)(2,1)S(1)}, u32[]{:S(2)}, u32[]{:S(2)}) collective-permute-start(bf16[384,384]{1,0:T(8,128)(2,1)S(1)} %get-tuple-element.43), channel_id=1, source_target_pairs={{6,7},{14,15},{22,23},{30,14},{12,4},{21,13}} | collective-permute-start | bytes 884744 | tf_op jit(solution)/shard_map/ppermute | solution.py:248
  (10 other events, 9.6 us)
